TPU v7x, 256 devices: a whole 4x4x8 slice. The times are simulated.
256 devices in a mesh: lat: 8 (over z_hi, core), lon: 32 (over x, z_lo, y).
Axes of the slice: x: 4, y: 4, z: 8 (z_hi: 4, z_lo: 2; z = z_hi * 2 + z_lo), core: 2. Of those that a mesh axis runs over, the one named last changes fastest.
Arguments:
- forcing: bfloat16 [16, 128, 4096], P(None, 'lat', 'lon'), may hold values from -6 to 6
- hidden: bfloat16 [64, 128, 4096], P(None, 'lat', 'lon'), may hold values from -3 to 3
- cell: bfloat16 [64, 128, 4096], P(None, 'lat', 'lon'), may hold values from -6 to 6
- grad_hidden: bfloat16 [64, 128, 4096], P(None, 'lat', 'lon'), may hold values from -6 to 6
- grad_cell: bfloat16 [64, 128, 4096], P(None, 'lat', 'lon'), may hold values from -6 to 6
- wet_mask: int32 [8, 256], P('lat'), may hold values from 0 to 1
- tile_owner: int32 [8, 256], P('lat'), may hold values from 0 to 31, as said below
- w_gates: bfloat16 [256, 720], replicated, may hold values from -0.21875 to 0.21875
- b_gates: float32 [256], replicated, may hold values from -3 to 3
Outputs:
- hidden_next: bfloat16 [64, 128, 4096], P(None, 'lat', 'lon')
- cell_next: float32 [1024, 64, 256], P(('lat', 'lon'))
- hidden_grad: float32 [64, 128, 4096], P(None, 'lat', 'lon')
- cell_grad: float32 [64, 128, 4096], P(None, 'lat', 'lon')
- weight_grad: float32 [256, 720], replicated
- bias_grad: float32 [256], replicated
Inputs may be any that keep to these rules, and one draw needn't show every extreme that they name: Within each group of 1 tile rows, tile_owner gives every longitude index exactly 4 wet tiles, and gives the wet tiles of one longitude block of 8 tile columns at most 1 to any one index; both bounds are reached in every draw, and some block is wet throughout. Dry tiles carry an owner too.
All inputs are finite; a program needn't handle non-finite values.
Results may differ from a plain program's by a relative error of at most 0.0033.
Values may be sent and summed in bfloat16 or wider, within the bound.
A program may use at most 64 MiB of HBM per device.

v0:
```python
import math
import jax
import jax.numpy as jnp
from jax import lax
from jax.sharding import PartitionSpec as P

TILE = 16


def extended_2(cells, sides, width):
    for axis, dim in sides:
        count = lax.axis_size(axis)
        head = lax.slice_in_dim(cells, 0, width, axis=dim)
        tail = lax.slice_in_dim(cells, cells.shape[dim] - width, cells.shape[dim], axis=dim)
        cells = jnp.concatenate(
            [
                lax.ppermute(tail, axis, [(i, (i + 1) % count) for i in range(count)]),
                cells,
                lax.ppermute(head, axis, [((i + 1) % count, i) for i in range(count)]),
            ],
            axis=dim,
        )
    return cells


def last_pad(values_in, pad_front, pad_back):
    widths = [(0, 0)] * (values_in.ndim - 1) + [(pad_front, pad_back)]
    return jnp.pad(values_in, widths)


def fold_edges(values_in):
    tile_count = values_in.shape[-2]
    inner_size = values_in.shape[-1] - 2
    leading = values_in.shape[:-2]
    flat_shape = leading + (tile_count * inner_size,)
    middle = values_in[..., 1 : inner_size + 1].reshape(flat_shape)
    zeros_left = jnp.zeros(leading + (tile_count, inner_size - 1), values_in.dtype)
    left_edge = jnp.concatenate([values_in[..., 0:1], zeros_left], -1).reshape(flat_shape)
    zeros_one = jnp.zeros(leading + (tile_count, 1), values_in.dtype)
    zeros_rest = jnp.zeros(leading + (tile_count, inner_size - 2), values_in.dtype)
    right_edge = jnp.concatenate(
        [zeros_one, values_in[..., inner_size + 1 : inner_size + 2], zeros_rest], -1
    ).reshape(flat_shape)
    full_size = tile_count * inner_size + 2
    return (
        last_pad(middle, 1, 1)
        + last_pad(left_edge, 0, 2)
        + last_pad(right_edge, inner_size, 0)[..., :full_size]
    )


def lstm_terms(pre_in, pre_forget, pre_out, pre_cand, cell_in, hidden_cot, cell_cot, live_cells):
    gate_in = jax.nn.sigmoid(pre_in)
    gate_forget = jax.nn.sigmoid(pre_forget)
    gate_out = jax.nn.sigmoid(pre_out)
    candidate = jnp.tanh(pre_cand)
    cell_new = gate_forget * cell_in + gate_in * candidate
    squash = jnp.tanh(cell_new)
    hidden_new = (live_cells * gate_out * squash).astype(jnp.bfloat16)
    back_h = live_cells * hidden_cot.astype(jnp.float32)
    back_c = live_cells * cell_cot.astype(jnp.float32) + back_h * gate_out * (1.0 - squash * squash)
    cell_back = back_c * gate_forget
    delta_parts = (
        back_c * candidate * gate_in * (1.0 - gate_in),
        back_c * cell_in * gate_forget * (1.0 - gate_forget),
        back_h * squash * gate_out * (1.0 - gate_out),
        back_c * gate_in * (1.0 - candidate * candidate),
    )
    return (hidden_new, cell_new, cell_back, delta_parts)


def tile_step(slab_tiles, cell_tiles, hidden_cot, cell_cot, live_tiles, w_gates, b_gates):
    tile_count = slab_tiles.shape[0]
    channels = slab_tiles.shape[1]
    hid_count = cell_tiles.shape[1]
    side_cells = TILE
    tile_grid = slab_tiles.reshape(tile_count, channels, side_cells + 2, side_cells + 2)
    tap_list = []
    for row_off in range(3):
        for col_off in range(3):
            tap_list.append(
                tile_grid[
                    :, :, row_off : row_off + side_cells, col_off : col_off + side_cells
                ].reshape(tile_count, channels, side_cells * side_cells)
            )
    patches = jnp.concatenate(tap_list, 1)
    pre_gates = (
        jnp.einsum("gk,nkc->ngc", w_gates, patches, preferred_element_type=jnp.float32)
        + b_gates[None, :, None]
    )
    live_cells = live_tiles[:, None, None]
    hidden_new, cell_new, cell_back, delta_parts = lstm_terms(
        pre_gates[:, :hid_count],
        pre_gates[:, hid_count : 2 * hid_count],
        pre_gates[:, 2 * hid_count : 3 * hid_count],
        pre_gates[:, 3 * hid_count :],
        cell_tiles.astype(jnp.float32),
        hidden_cot,
        cell_cot,
        live_cells,
    )
    gate_delta = jnp.concatenate(delta_parts, 1).astype(jnp.bfloat16)
    weight_part = jnp.einsum("ngc,nkc->gk", gate_delta, patches, preferred_element_type=jnp.float32)
    bias_part = jnp.sum(gate_delta.astype(jnp.float32), axis=(0, 2))
    hid_weights = w_gates.reshape(w_gates.shape[0], 9, channels)[:, :, channels - hid_count :]
    spread = jnp.einsum(
        "gth,ngc->nthc", hid_weights, gate_delta, preferred_element_type=jnp.float32
    )
    grad_pad = jnp.zeros((tile_count, hid_count, side_cells + 2, side_cells + 2), jnp.float32)
    for row_off in range(3):
        for col_off in range(3):
            placed = spread[:, row_off * 3 + col_off].reshape(
                tile_count, hid_count, side_cells, side_cells
            )
            grad_pad = grad_pad + jnp.pad(
                placed, ((0, 0), (0, 0), (row_off, 2 - row_off), (col_off, 2 - col_off))
            )
    grad_pad = grad_pad.reshape(tile_count, hid_count, (side_cells + 2) * (side_cells + 2))
    return (hidden_new, cell_new, cell_back, grad_pad, weight_part, bias_part)


def outside_rows(row_total, lat_index, lat_devices):
    position = jnp.arange(row_total, dtype=jnp.int32)
    upper = (position == 0) & (lat_index == 0)
    lower = (position == row_total - 1) & (lat_index == lat_devices - 1)
    return jnp.where(upper | lower, 0.0, 1.0).astype(jnp.float32)


def cut_tiles(padded, tile_rows, tile_cols):
    channels = padded.shape[0]
    side_cells = TILE + 2
    row_pick = (
        jnp.arange(tile_rows, dtype=jnp.int32)[:, None] * TILE
        + jnp.arange(side_cells, dtype=jnp.int32)[None, :]
    ).reshape(-1)
    col_pick = (
        jnp.arange(tile_cols, dtype=jnp.int32)[:, None] * TILE
        + jnp.arange(side_cells, dtype=jnp.int32)[None, :]
    ).reshape(-1)
    strips = jnp.take(padded, row_pick, axis=1).reshape(
        channels, tile_rows, side_cells, padded.shape[2]
    )
    pieces = jnp.take(strips, col_pick, axis=3).reshape(
        channels, tile_rows, side_cells, tile_cols, side_cells
    )
    return jnp.transpose(pieces, (1, 3, 0, 2, 4)).reshape(
        tile_rows * tile_cols, channels, side_cells * side_cells
    )


def to_tiles(values_in, tile_rows, tile_cols):
    channels = values_in.shape[0]
    shaped = values_in.reshape(channels, tile_rows, TILE, tile_cols, TILE)
    return jnp.transpose(shaped, (1, 3, 0, 2, 4)).reshape(
        tile_rows * tile_cols, channels, TILE * TILE
    )


def from_tiles(tiles_in, tile_rows, tile_cols):
    channels = tiles_in.shape[1]
    shaped = tiles_in.reshape(tile_rows, tile_cols, channels, TILE, TILE)
    return jnp.transpose(shaped, (2, 0, 3, 1, 4)).reshape(
        channels, tile_rows * TILE, tile_cols * TILE
    )


def sender_plan(wet_local, dest_local, slot_count, pair_most):
    tile_count = wet_local.shape[0]
    position = jnp.arange(tile_count, dtype=jnp.int32)
    earlier = position[:, None] < position[None, :]
    same_dest = (
        (dest_local[:, None] == dest_local[None, :]) & wet_local[:, None] & wet_local[None, :]
    )
    dest_rank = jnp.sum((same_dest & earlier).astype(jnp.int32), 0)
    slot_of = dest_local * pair_most + dest_rank
    placed = wet_local[:, None] & (
        slot_of[:, None] == jnp.arange(slot_count, dtype=jnp.int32)[None, :]
    )
    source = jnp.sum(placed.astype(jnp.int32) * position[:, None], 0)
    filled = jnp.any(placed, 0)
    send_index = jnp.where(filled, source, tile_count)
    home_index = jnp.where(wet_local, slot_of, slot_count)
    return (send_index, home_index)


def receiver_plan(arrivals, pair_most, capacity):
    slot_count = arrivals.shape[0] * pair_most
    positions = jnp.arange(slot_count, dtype=jnp.int32)
    filled = positions % pair_most < jnp.repeat(arrivals, pair_most)
    slot_rank = jnp.cumsum(filled.astype(jnp.int32)) - 1
    placed = filled[None, :] & (
        slot_rank[None, :] == jnp.arange(capacity, dtype=jnp.int32)[:, None]
    )
    work_index = jnp.sum(placed.astype(jnp.int32) * positions[None, :], 1)
    back_index = jnp.where(filled, slot_rank, capacity)
    return (work_index, back_index)


def pick_rows(arrays, row_index):
    picked = []
    for member in arrays:
        extended = jnp.concatenate([member, jnp.zeros((1,) + member.shape[1:], member.dtype)], 0)
        picked.append(jnp.take(extended, row_index, axis=0))
    return tuple(picked)


def fold_grad(pad_tiles, tile_rows, tile_cols, row_keep):
    hid_count = pad_tiles.shape[1]
    side_cells = TILE + 2
    shaped = pad_tiles.reshape(tile_rows, tile_cols, hid_count, side_cells, side_cells)
    across = fold_edges(jnp.transpose(shaped, (0, 2, 3, 1, 4)))
    down_fold = fold_edges(jnp.transpose(across, (1, 3, 0, 2)))
    overhang = jnp.transpose(down_fold, (0, 2, 1)) * row_keep[None, :, None]
    received = extended_2(overhang, (("lat", 1), ("lon", 2)), 1)
    lat_size = overhang.shape[1] - 2
    lon_size = overhang.shape[2] - 2
    columns = received[:, :, 2 : lon_size + 2]
    columns = columns.at[:, :, 0].add(received[:, :, 0])
    columns = columns.at[:, :, lon_size - 1].add(received[:, :, lon_size + 3])
    result = columns[:, 2 : lat_size + 2]
    result = result.at[:, 0].add(columns[:, 0])
    result = result.at[:, lat_size - 1].add(columns[:, lat_size + 3])
    return result


def body(forcing, hidden, cell, grad_hidden, grad_cell, wet_mask, tile_owner, w_gates, b_gates):
    lat_index = lax.axis_index("lat")
    lon_index = lax.axis_index("lon")
    lat_devices = lax.axis_size("lat")
    lon_devices = lax.axis_size("lon")
    tile_rows = wet_mask.shape[0]
    tile_cols = wet_mask.shape[1] // lon_devices
    tile_count = tile_rows * tile_cols
    pair_most = max(1, tile_count // lon_devices)
    slot_count = lon_devices * pair_most
    capacity = tile_count // 2
    fields = jnp.concatenate([forcing, hidden], 0)
    padded = extended_2(fields, (("lat", 1), ("lon", 2)), 1)
    row_keep = outside_rows(padded.shape[1], lat_index, lat_devices)
    padded = padded * row_keep.astype(jnp.bfloat16)[None, :, None]
    slab_tiles = cut_tiles(padded, tile_rows, tile_cols)
    cell_tiles = to_tiles(cell, tile_rows, tile_cols)
    hidden_cot = to_tiles(grad_hidden, tile_rows, tile_cols)
    cell_cot = to_tiles(grad_cell, tile_rows, tile_cols)
    wet_local = (
        lax.dynamic_slice_in_dim(wet_mask, lon_index * tile_cols, tile_cols, 1).reshape(tile_count)
        > 0
    )
    dest_local = lax.dynamic_slice_in_dim(tile_owner, lon_index * tile_cols, tile_cols, 1).reshape(
        tile_count
    )
    send_index, home_index = sender_plan(wet_local, dest_local, slot_count, pair_most)
    owned_here = (wet_mask > 0) & (tile_owner == lon_index)
    arrivals = jnp.sum(
        owned_here.reshape(tile_rows, lon_devices, tile_cols).astype(jnp.int32), axis=(0, 2)
    )
    work_index, back_index = receiver_plan(arrivals, pair_most, capacity)
    hid_tiles, cell_new, back_tiles, pad_tiles, weight_part, bias_part = tile_step(
        slab_tiles,
        cell_tiles,
        hidden_cot,
        cell_cot,
        wet_local.astype(jnp.float32),
        w_gates,
        b_gates,
    )
    outgoing_state = pick_rows((cell_new,), send_index)[0]
    incoming_state = lax.all_to_all(outgoing_state, "lon", split_axis=0, concat_axis=0, tiled=True)
    cell_next = pick_rows((incoming_state,), work_index)[0]
    hidden_next = from_tiles(hid_tiles, tile_rows, tile_cols)
    cell_grad = from_tiles(back_tiles, tile_rows, tile_cols)
    hidden_grad = fold_grad(pad_tiles, tile_rows, tile_cols, row_keep)
    totals = lax.psum((weight_part, bias_part), ("lat", "lon"))
    scaling = 1.0 / math.sqrt(float(lat_devices * lon_devices * capacity * TILE * TILE))
    return (
        hidden_next,
        cell_next,
        hidden_grad,
        cell_grad,
        totals[0] * scaling,
        totals[1] * scaling,
    )


def solution(mesh):
    return jax.shard_map(
        body,
        mesh=mesh,
        in_specs=(
            P(None, "lat", "lon"),
            P(None, "lat", "lon"),
            P(None, "lat", "lon"),
            P(None, "lat", "lon"),
            P(None, "lat", "lon"),
            P("lat", None),
            P("lat", None),
            P(),
            P(),
        ),
        out_specs=(
            P(None, "lat", "lon"),
            P(("lat", "lon"), None, None),
            P(None, "lat", "lon"),
            P(None, "lat", "lon"),
            P(),
            P(),
        ),
        check_vma=False,
    )
```

profile of v0, /device:TPU:6, one launch (start us, length us, event | category | flops | bytes accessed | tf_op | source)
XLA Modules:
  0.0 355.3 jit_solution(3883284366061151006)
XLA Ops:
  9.9 5.8 %collective-permute-start.1 = (bf16[80,1,128]{0,2,1:T(8,128)(2,1)S(1)}, bf16[80,1,128]{0,2,1:T(8,128)(2,1)S(1)}, u32[]{:S(2)}, u32[]{:S(2)}) collective-permute-start(bf16[80,1,128]{0,2,1:T(8,128)(2,1)S(1)} %get-tuple-element.100), channel_id=1, source_target_pairs={{32,0},{64,32},{96,64},{128,96},{160,128},{192,160},{224,192},{0,2... | collective-permute-start | bytes 61448 | tf_op jit(solution)/shard_map/ppermute | solution.py:19
  23.1 3.5 collective-permute-start.3
  29.3 2.3 copy.109
  34.2 2.4 copy.107
  75.4 5.6 %all-to-all-start = ((f32[32,64,256]{2,1,0:T(8,128)}), f32[32,64,256]{2,1,0:T(8,128)S(1)}, u32[]{:S(2)}, u32[]{:S(2)}) async-start(f32[32,64,256]{2,1,0:T(8,128)} %broadcast_select_fusion), calls=%async_computation | async-start | bytes 4194304 | tf_op jit(solution)/shard_map/all_to_all | solution.py:268
  82.8 2.2 fusion.32
  86.4 2.3 copy.120
  88.7 2.4 copy.119
  91.1 2.4 copy.118
  93.5 2.4 copy.117
  95.9 2.4 copy.116
  98.3 2.4 copy.115
  100.7 2.4 copy.114
  103.1 2.4 copy.113
  105.5 4.7 %add_bitcast_fusion.1 = f32[1,64,18,8,18]{1,4,2,3,0:T(8,128)S(1)} fusion(f32[8,64,16,16]{1,3,2,0:T(8,128)} %bitcast.122, f32[8,64,16,16]{1,3,2,0:T(8,128)} %bitcast.123, f32[8,64,16,16]{1,3,2,0:T(8,128)} %bitcast.124, f32[8,64,16,16]{1,3,2,0:T(8,128)} %bitcast.125, f32[8,64,16,16]{1,3,2,0:T(8,128)} %bitcast.126, f32[8,64,16,16]{1,3,2,0:T(8,128)} %bitcast.127, ...), kind=kLoop, calls=%fused_computation.8 | loop fusion | flops 1327104 | bytes 5382144 | tf_op jit(solution)/shard_map/transpose | solution.py:211
  112.5 3.9 %collective-permute-start.5 = (f32[64,1,130]{0,2,1:T(8,128)}, f32[64,1,130]{0,2,1:T(8,128)S(1)}, u32[]{:S(2)}, u32[]{:S(2)}) collective-permute-start(f32[64,1,130]{0,2,1:T(8,128)} %get-tuple-element.94), channel_id=1, source_target_pairs={{32,0},{64,32},{96,64},{128,96},{160,128},{192,160},{224,192},{0,2... | collective-permute-start | bytes 99848 | tf_op jit(solution)/shard_map/ppermute | solution.py:19
  116.6 75.5 %psum.15 = f32[256]{0:T(256)S(1)} all-reduce(f32[256]{0:T(256)S(1)} %convert_reduce_fusion), channel_id=1, replica_groups=mesh['lat'=8,'lon'=32] {'lat','lon'}, use_global_device_ids=true, to_apply=%region_8.9 | all-reduce | flops 256 | bytes 2048 | tf_op jit(solution)/shard_map/psum | solution.py:273
  198.5 2.3 copy.124
  200.9 2.4 copy.125
  203.2 2.4 copy.128
  209.0 4.0 %collective-permute-done.6 = f32[64,20,1]{0,2,1:T(1,128)S(1)} collective-permute-done((f32[64,20,1]{0,2,1:T(1,128)S(1)}, f32[64,20,1]{0,2,1:T(1,128)S(1)}, u32[]{:S(2)}, u32[]{:S(2)}) %collective-permute-start.6) | collective-permute-done | bytes 5152 | tf_op jit(solution)/shard_map/ppermute | solution.py:17
  221.4 120.5 %all-reduce.19.cloned.1.call-done = f32[256,720]{0,1:T(8,128)} async-done(((f32[256,720]{0,1:T(8,128)}), f32[256,720]{0,1:T(8,128)}) %all-reduce.19.cloned.1.call-update) | async-done | bytes 737296 | tf_op jit(solution)/shard_map/psum | solution.py:273
  341.9 2.0 broadcast_multiply_fusion
  345.5 2.2 gather_fusion.3
  (178 shorter events, 79.8 us)
Async XLA Ops:
  7.2 8.5 %copy-start.20 = (s32[1,256]{1,0:T(1,128)S(1)}, s32[1,256]{1,0:T(1,128)}, u32[]{:S(2)}) copy-start(s32[1,256]{1,0:T(1,128)} %param.23) | copy-start | bytes 3076
  7.2 8.5 %copy-start.19 = (s32[1,256]{1,0:T(1,128)S(1)}, s32[1,256]{1,0:T(1,128)}, u32[]{:S(2)}) copy-start(s32[1,256]{1,0:T(1,128)} %param.22) | copy-start | bytes 3076
  7.2 9.9 %copy-start.15 = (bf16[64,16,128]{2,1,0:T(8,128)(2,1)S(1)}, bf16[64,16,128]{2,1,0:T(8,128)(2,1)}, u32[]{:S(2)}) copy-start(bf16[64,16,128]{2,1,0:T(8,128)(2,1)} %param.19) | copy-start | bytes 786436
  7.2 334.7 %all-reduce.19.cloned.1.call-start = ((), (), s32[]{:S(2)}) async-start(), calls=%async_computation.1 | async-start | bytes 1474560 | tf_op jit(solution)/shard_map/psum | solution.py:273
  9.7 7.9 %copy-start.16 = (bf16[64,16,128]{2,1,0:T(8,128)(2,1)S(1)}, bf16[64,16,128]{2,1,0:T(8,128)(2,1)}, u32[]{:S(2)}) copy-start(bf16[64,16,128]{2,1,0:T(8,128)(2,1)} %param.20) | copy-start | bytes 786436
  9.8 11.5 %collective-permute-start = (bf16[80,1,128]{0,2,1:T(8,128)(2,1)S(1)}, bf16[80,1,128]{0,2,1:T(8,128)(2,1)S(1)}, u32[]{:S(2)}, u32[]{:S(2)}) collective-permute-start(bf16[80,1,128]{0,2,1:T(8,128)(2,1)S(1)} %get-tuple-element.99), channel_id=1, source_target_pairs={{0,32},{32,64},{64,96},{96,128},{128,160},{160,192},{192,224},{224... | collective-permute-start | bytes 61448 | tf_op jit(solution)/shard_map/ppermute | solution.py:17
  9.9 11.5 %collective-permute-start.1 = (bf16[80,1,128]{0,2,1:T(8,128)(2,1)S(1)}, bf16[80,1,128]{0,2,1:T(8,128)(2,1)S(1)}, u32[]{:S(2)}, u32[]{:S(2)}) collective-permute-start(bf16[80,1,128]{0,2,1:T(8,128)(2,1)S(1)} %get-tuple-element.100), channel_id=1, source_target_pairs={{32,0},{64,32},{96,64},{128,96},{160,128},{192,160},{224,192},{0,2... | collective-permute-start | bytes 61448 | tf_op jit(solution)/shard_map/ppermute | solution.py:19
  21.4 15.2 %collective-permute-start.2 = (bf16[80,18,1]{0,2,1:T(2,128)(2,1)S(1)}, bf16[80,18,1]{0,2,1:T(2,128)(2,1)S(1)}, u32[]{:S(2)}, u32[]{:S(2)}) collective-permute-start(bf16[80,18,1]{0,2,1:T(2,128)(2,1)S(1)} %get-tuple-element.97), channel_id=1, source_target_pairs={{0,1},{1,2},{2,3},{3,4},{4,5},{5,6},{6,7},{7,8},{8,9},{9,10},{10,1... | collective-permute-start | bytes 8648 | tf_op jit(solution)/shard_map/ppermute | solution.py:17
  23.1 13.5 %collective-permute-start.3 = (bf16[80,18,1]{0,2,1:T(2,128)(2,1)S(1)}, bf16[80,18,1]{0,2,1:T(2,128)(2,1)S(1)}, u32[]{:S(2)}, u32[]{:S(2)}) collective-permute-start(bf16[80,18,1]{0,2,1:T(2,128)(2,1)S(1)} %get-tuple-element.98), channel_id=1, source_target_pairs={{1,0},{2,1},{3,2},{4,3},{5,4},{6,5},{7,6},{8,7},{9,8},{10,9},{11,1... | collective-permute-start | bytes 8648 | tf_op jit(solution)/shard_map/ppermute | solution.py:19
  63.2 3.0 copy-start.13
  71.2 9.8 %copy-start = (bf16[8,64,256]{2,1,0:T(8,128)(2,1)}, bf16[8,64,256]{2,1,0:T(8,128)(2,1)S(1)}, u32[]{:S(2)}) copy-start(bf16[8,64,256]{2,1,0:T(8,128)(2,1)S(1)} %get-tuple-element.84) | copy-start | bytes 786436
  71.2 9.8 %copy-start.2 = (bf16[8,64,256]{2,1,0:T(8,128)(2,1)}, bf16[8,64,256]{2,1,0:T(8,128)(2,1)S(1)}, u32[]{:S(2)}) copy-start(bf16[8,64,256]{2,1,0:T(8,128)(2,1)S(1)} %get-tuple-element.85) | copy-start | bytes 786436
  71.2 9.8 %copy-start.4 = (bf16[8,64,256]{2,1,0:T(8,128)(2,1)}, bf16[8,64,256]{2,1,0:T(8,128)(2,1)S(1)}, u32[]{:S(2)}) copy-start(bf16[8,64,256]{2,1,0:T(8,128)(2,1)S(1)} %get-tuple-element.86) | copy-start | bytes 786436
  75.4 5.7 %copy-start.7 = (bf16[8,64,256]{2,1,0:T(8,128)(2,1)S(1)}, bf16[8,64,256]{2,1,0:T(8,128)(2,1)}, u32[]{:S(2)}) copy-start(bf16[8,64,256]{2,1,0:T(8,128)(2,1)} %copy-done.6) | copy-start | bytes 786436
  75.4 268.5 %all-to-all-start = ((f32[32,64,256]{2,1,0:T(8,128)}), f32[32,64,256]{2,1,0:T(8,128)S(1)}, u32[]{:S(2)}, u32[]{:S(2)}) async-start(f32[32,64,256]{2,1,0:T(8,128)} %broadcast_select_fusion), calls=%async_computation | async-start | bytes 4194304 | tf_op jit(solution)/shard_map/all_to_all | solution.py:268
  105.5 4.8 %copy-start.21 = (pred[16]{0:T(512)(128)(4,1)S(1)}, pred[16]{0:T(512)(128)(4,1)}, u32[]{:S(2)}) copy-start(pred[16]{0:T(512)(128)(4,1)} %constant.228.clone.1) | copy-start | bytes 52
  111.6 4.8 %copy-start.1 = (bf16[8,64,256]{2,1,0:T(8,128)(2,1)S(1)}, bf16[8,64,256]{2,1,0:T(8,128)(2,1)}, u32[]{:S(2)}) copy-start(bf16[8,64,256]{2,1,0:T(8,128)(2,1)} %copy-done) | copy-start | bytes 786436
  111.6 4.8 %copy-start.3 = (bf16[8,64,256]{2,1,0:T(8,128)(2,1)S(1)}, bf16[8,64,256]{2,1,0:T(8,128)(2,1)}, u32[]{:S(2)}) copy-start(bf16[8,64,256]{2,1,0:T(8,128)(2,1)} %copy-done.2) | copy-start | bytes 786436
  111.6 4.7 %copy-start.5 = (bf16[8,64,256]{2,1,0:T(8,128)(2,1)S(1)}, bf16[8,64,256]{2,1,0:T(8,128)(2,1)}, u32[]{:S(2)}) copy-start(bf16[8,64,256]{2,1,0:T(8,128)(2,1)} %copy-done.4) | copy-start | bytes 786436
  111.7 4.7 %copy-start.8 = (bf16[8,64,256]{2,1,0:T(8,128)(2,1)S(1)}, bf16[8,64,256]{2,1,0:T(8,128)(2,1)}, u32[]{:S(2)}) copy-start(bf16[8,64,256]{2,1,0:T(8,128)(2,1)} %copy-done.6) | copy-start | bytes 786436
  112.5 93.1 %collective-permute-start.4 = (f32[64,1,130]{0,2,1:T(8,128)}, f32[64,1,130]{0,2,1:T(8,128)S(1)}, u32[]{:S(2)}, u32[]{:S(2)}) collective-permute-start(f32[64,1,130]{0,2,1:T(8,128)} %get-tuple-element.93), channel_id=1, source_target_pairs={{0,32},{32,64},{64,96},{96,128},{128,160},{160,192},{192,224},{224... | collective-permute-start | bytes 99848 | tf_op jit(solution)/shard_map/ppermute | solution.py:17
  112.5 93.1 %collective-permute-start.5 = (f32[64,1,130]{0,2,1:T(8,128)}, f32[64,1,130]{0,2,1:T(8,128)S(1)}, u32[]{:S(2)}, u32[]{:S(2)}) collective-permute-start(f32[64,1,130]{0,2,1:T(8,128)} %get-tuple-element.94), channel_id=1, source_target_pairs={{32,0},{64,32},{96,64},{128,96},{160,128},{192,160},{224,192},{0,2... | collective-permute-start | bytes 99848 | tf_op jit(solution)/shard_map/ppermute | solution.py:19
  205.6 9.1 %collective-permute-start.7 = (f32[64,20,1]{0,2,1:T(1,128)S(1)}, f32[64,20,1]{0,2,1:T(1,128)S(1)}, u32[]{:S(2)}, u32[]{:S(2)}) collective-permute-start(f32[64,20,1]{0,2,1:T(1,128)S(1)} %get-tuple-element.91), channel_id=1, source_target_pairs={{1,0},{2,1},{3,2},{4,3},{5,4},{6,5},{7,6},{8,7},{9,8},{10,9},{11,1... | collective-permute-start | bytes 15368 | tf_op jit(solution)/shard_map/ppermute | solution.py:19
  206.4 6.7 %collective-permute-start.6 = (f32[64,20,1]{0,2,1:T(1,128)S(1)}, f32[64,20,1]{0,2,1:T(1,128)S(1)}, u32[]{:S(2)}, u32[]{:S(2)}) collective-permute-start(f32[64,20,1]{0,2,1:T(1,128)S(1)} %get-tuple-element.92), channel_id=1, source_target_pairs={{0,1},{1,2},{2,3},{3,4},{4,5},{5,6},{6,7},{7,8},{8,9},{9,10},{10,1... | collective-permute-start | bytes 15368 | tf_op jit(solution)/shard_map/ppermute | solution.py:17
  (9 other events, 14.7 us)
Sparse Core Ops, SparseCore 0:
  73.2 268.5 all-reduce.18
where the time goes:
time: 357 us; the launch traced here: 355 us
  waiting for transfers between devices  125 us (35%)
  local copies, waits for them, and re-layouts  92 us (26%)
  blocking collectives  75.5 us (21%)
  starting transfers between devices  22.7 us (6%)
  other arithmetic  21.3 us (6%)
  between operations  14.7 us (4%)
  matrix products  4.63 us (1%)
    psum x1, waiting for transfers between devices, body(): totals = lax.psum((weight_part, bias_part), ('lat', 'lon'))  120 us
    psum x1, blocking collectives, body(): totals = lax.psum((weight_part, bias_part), ('lat', 'lon'))  75.5 us
    slice x10, local copies, waits for them, and re-layouts, tile_step(): spread[:, row_off * 3 + col_off]  22.7 us
    ppermute x4, starting transfers between devices, extended_2(): lax.ppermute(head, axis, [((i + 1) % count, i) for i in range(count)])  13.9 us
    unnamed x62, local copies, waits for them, and re-layouts  13.4 us
    reshape x9, local copies, waits for them, and re-layouts, tile_step(): tap_list.append(tile_grid[:, :, row_off:row_off + side_cells, col_off:col...  13.1 us
    slice x10, local copies, waits for them, and re-layouts, tile_step(): tile_grid[:, :, row_off:row_off + side_cells, col_off:col_off + side_cells]  11.2 us
  transfers between devices with their start and end apart: 10, of which 2 were waited for; matrix products, arithmetic and copies ran while one was open for 21% of the time, Pallas kernels for 0%

commit v1 on v0

--- a/solution.py
+++ b/solution.py
@@ -270,7 +270,7 @@
     hidden_next = from_tiles(hid_tiles, tile_rows, tile_cols)
     cell_grad = from_tiles(back_tiles, tile_rows, tile_cols)
     hidden_grad = fold_grad(pad_tiles, tile_rows, tile_cols, row_keep)
-    totals = lax.psum((weight_part, bias_part), ("lat", "lon"))
+    totals = lax.psum(lax.psum((weight_part, bias_part), axis_name="lon"), axis_name="lat")
     scaling = 1.0 / math.sqrt(float(lat_devices * lon_devices * capacity * TILE * TILE))
     return (
         hidden_next,

time: 357 us -> 486 us (1.36)
  waiting for transfers between devices: 125 us -> 243 us
  blocking collectives: 75.5 us -> 85.3 us
    psum x1 -> x2, waiting for transfers between devices: 120 us -> 243 us  [the longest x1 166 us: body(): lax.psum((weight_part, bias_part), axis_name='lon')]
    psum x1 -> x2, blocking collectives: 75.5 us -> 85.3 us  [the longest x1 71.1 us: body(): lax.psum((weight_part, bias_part), axis_name='lon')]
  transfers between devices with their start and end apart: 10 -> 11, of which waited for: 2 -> 2; matrix products, arithmetic and copies ran while one was open for 21% -> 15% of each run, Pallas kernels for 0% -> 0%
where the time goes in v1:
time: 486 us; the launch traced here: 484 us
  waiting for transfers between devices  243 us (50%)
  local copies, waits for them, and re-layouts  91.9 us (19%)
  blocking collectives  85.3 us (18%)
  starting transfers between devices  22.9 us (5%)
  other arithmetic  21.2 us (4%)
  between operations  14.7 us (3%)
    psum x1, waiting for transfers between devices, body(): lax.psum((weight_part, bias_part), axis_name='lon')  166 us
    psum x1, waiting for transfers between devices, body(): lax.psum(lax.psum((weight_part, bias_part), axis_name='lon'), axis_name='...  76.7 us
    psum x1, blocking collectives, body(): lax.psum((weight_part, bias_part), axis_name='lon')  71.1 us
    slice x10, local copies, waits for them, and re-layouts, tile_step(): spread[:, row_off * 3 + col_off]  22.6 us
    psum x1, blocking collectives, body(): lax.psum(lax.psum((weight_part, bias_part), axis_name='lon'), axis_name='...  14.2 us
    unnamed x62, local copies, waits for them, and re-layouts  13.4 us
    ppermute x4, starting transfers between devices, extended_2(): lax.ppermute(head, axis, [((i + 1) % count, i) for i in range(count)])  13.4 us
    reshape x9, local copies, waits for them, and re-layouts, tile_step(): tap_list.append(tile_grid[:, :, row_off:row_off + side_cells, col_off:col...  13.1 us
  transfers between devices with their start and end apart: 11, of which 2 were waited for; matrix products, arithmetic and copies ran while one was open for 15% of the time, Pallas kernels for 0%

profile of v1, /device:TPU:6, one launch (start us, length us, event | category | flops | bytes accessed | tf_op | source)
XLA Modules:
  0.0 483.6 jit_solution(11682873963150306942)
XLA Ops:
  9.9 5.8 %collective-permute-start.1 = (bf16[80,1,128]{0,2,1:T(8,128)(2,1)S(1)}, bf16[80,1,128]{0,2,1:T(8,128)(2,1)S(1)}, u32[]{:S(2)}, u32[]{:S(2)}) collective-permute-start(bf16[80,1,128]{0,2,1:T(8,128)(2,1)S(1)} %get-tuple-element.100), channel_id=1, source_target_pairs={{32,0},{64,32},{96,64},{128,96},{160,128},{192,160},{224,192},{0,2... | collective-permute-start | bytes 61448 | tf_op jit(solution)/shard_map/ppermute | solution.py:19
  23.1 3.5 collective-permute-start.3
  29.3 2.3 copy.109
  34.2 2.4 copy.107
  75.4 5.6 %all-to-all-start = ((f32[32,64,256]{2,1,0:T(8,128)}), f32[32,64,256]{2,1,0:T(8,128)S(1)}, u32[]{:S(2)}, u32[]{:S(2)}) async-start(f32[32,64,256]{2,1,0:T(8,128)} %broadcast_select_fusion), calls=%async_computation | async-start | bytes 4194304 | tf_op jit(solution)/shard_map/all_to_all | solution.py:268
  83.1 2.2 fusion.32
  86.7 2.4 copy.120
  89.0 2.4 copy.119
  91.4 2.4 copy.118
  93.7 2.4 copy.117
  96.1 2.4 copy.116
  98.5 2.4 copy.115
  100.9 2.4 copy.114
  103.4 2.3 copy.113
  105.7 4.7 add_bitcast_fusion.1
  112.7 3.9 collective-permute-start.5
  116.8 71.1 %psum.30 = f32[256]{0:T(256)S(1)} all-reduce(f32[256]{0:T(256)S(1)} %convert_reduce_fusion), channel_id=1, replica_groups=mesh['lat'=8,'lon'=32] {'lon'}, use_global_device_ids=true, to_apply=%region_9.10 | all-reduce | flops 256 | bytes 2048 | tf_op jit(solution)/shard_map/psum | solution.py:273
  187.9 14.2 %psum.31 = f32[256]{0:T(256)S(1)} all-reduce(f32[256]{0:T(256)S(1)} %psum.30), channel_id=1, replica_groups=mesh['lat'=8,'lon'=32] {'lat'}, use_global_device_ids=true, to_apply=%region_10.11 | all-reduce | flops 256 | bytes 2048 | tf_op jit(solution)/shard_map/psum | solution.py:273
  208.5 2.3 copy.124
  210.8 2.3 copy.125
  213.2 2.4 copy.128
  219.0 166.3 %all-reduce.20.cloned.1.call-done = f32[256,720]{0,1:T(8,128)} async-done(((f32[256,720]{0,1:T(8,128)}), f32[256,720]{0,1:T(8,128)}) %all-reduce.20.cloned.1.call-update) | async-done | bytes 737296 | tf_op jit(solution)/shard_map/psum | solution.py:273
  393.5 76.7 %all-reduce.22.cloned.1.call-done = f32[256,720]{0,1:T(8,128)} async-done(((f32[256,720]{0,1:T(8,128)}), f32[256,720]{0,1:T(8,128)}) %all-reduce.22.cloned.1.call-update) | async-done | bytes 737296 | tf_op jit(solution)/shard_map/psum | solution.py:273
  473.8 2.2 gather_fusion.3
  (182 shorter events, 82.1 us)
Async XLA Ops:
  7.2 8.5 %copy-start.20 = (s32[1,256]{1,0:T(1,128)S(1)}, s32[1,256]{1,0:T(1,128)}, u32[]{:S(2)}) copy-start(s32[1,256]{1,0:T(1,128)} %param.23) | copy-start | bytes 3076
  7.2 8.5 %copy-start.19 = (s32[1,256]{1,0:T(1,128)S(1)}, s32[1,256]{1,0:T(1,128)}, u32[]{:S(2)}) copy-start(s32[1,256]{1,0:T(1,128)} %param.22) | copy-start | bytes 3076
  7.2 9.9 %copy-start.15 = (bf16[64,16,128]{2,1,0:T(8,128)(2,1)S(1)}, bf16[64,16,128]{2,1,0:T(8,128)(2,1)}, u32[]{:S(2)}) copy-start(bf16[64,16,128]{2,1,0:T(8,128)(2,1)} %param.19) | copy-start | bytes 786436
  7.2 378.1 %all-reduce.20.cloned.1.call-start = ((), (), s32[]{:S(2)}) async-start(), calls=%async_computation.1 | async-start | bytes 1474560 | tf_op jit(solution)/shard_map/psum | solution.py:273
  9.7 7.9 %copy-start.16 = (bf16[64,16,128]{2,1,0:T(8,128)(2,1)S(1)}, bf16[64,16,128]{2,1,0:T(8,128)(2,1)}, u32[]{:S(2)}) copy-start(bf16[64,16,128]{2,1,0:T(8,128)(2,1)} %param.20) | copy-start | bytes 786436
  9.8 11.5 %collective-permute-start = (bf16[80,1,128]{0,2,1:T(8,128)(2,1)S(1)}, bf16[80,1,128]{0,2,1:T(8,128)(2,1)S(1)}, u32[]{:S(2)}, u32[]{:S(2)}) collective-permute-start(bf16[80,1,128]{0,2,1:T(8,128)(2,1)S(1)} %get-tuple-element.99), channel_id=1, source_target_pairs={{0,32},{32,64},{64,96},{96,128},{128,160},{160,192},{192,224},{224... | collective-permute-start | bytes 61448 | tf_op jit(solution)/shard_map/ppermute | solution.py:17
  9.9 11.5 %collective-permute-start.1 = (bf16[80,1,128]{0,2,1:T(8,128)(2,1)S(1)}, bf16[80,1,128]{0,2,1:T(8,128)(2,1)S(1)}, u32[]{:S(2)}, u32[]{:S(2)}) collective-permute-start(bf16[80,1,128]{0,2,1:T(8,128)(2,1)S(1)} %get-tuple-element.100), channel_id=1, source_target_pairs={{32,0},{64,32},{96,64},{128,96},{160,128},{192,160},{224,192},{0,2... | collective-permute-start | bytes 61448 | tf_op jit(solution)/shard_map/ppermute | solution.py:19
  21.4 15.2 %collective-permute-start.2 = (bf16[80,18,1]{0,2,1:T(2,128)(2,1)S(1)}, bf16[80,18,1]{0,2,1:T(2,128)(2,1)S(1)}, u32[]{:S(2)}, u32[]{:S(2)}) collective-permute-start(bf16[80,18,1]{0,2,1:T(2,128)(2,1)S(1)} %get-tuple-element.97), channel_id=1, source_target_pairs={{0,1},{1,2},{2,3},{3,4},{4,5},{5,6},{6,7},{7,8},{8,9},{9,10},{10,1... | collective-permute-start | bytes 8648 | tf_op jit(solution)/shard_map/ppermute | solution.py:17
  23.1 13.5 %collective-permute-start.3 = (bf16[80,18,1]{0,2,1:T(2,128)(2,1)S(1)}, bf16[80,18,1]{0,2,1:T(2,128)(2,1)S(1)}, u32[]{:S(2)}, u32[]{:S(2)}) collective-permute-start(bf16[80,18,1]{0,2,1:T(2,128)(2,1)S(1)} %get-tuple-element.98), channel_id=1, source_target_pairs={{1,0},{2,1},{3,2},{4,3},{5,4},{6,5},{7,6},{8,7},{9,8},{10,9},{11,1... | collective-permute-start | bytes 8648 | tf_op jit(solution)/shard_map/ppermute | solution.py:19
  71.2 10.0 %copy-start = (bf16[8,64,256]{2,1,0:T(8,128)(2,1)}, bf16[8,64,256]{2,1,0:T(8,128)(2,1)S(1)}, u32[]{:S(2)}) copy-start(bf16[8,64,256]{2,1,0:T(8,128)(2,1)S(1)} %get-tuple-element.84) | copy-start | bytes 786436
  71.2 10.0 %copy-start.2 = (bf16[8,64,256]{2,1,0:T(8,128)(2,1)}, bf16[8,64,256]{2,1,0:T(8,128)(2,1)S(1)}, u32[]{:S(2)}) copy-start(bf16[8,64,256]{2,1,0:T(8,128)(2,1)S(1)} %get-tuple-element.85) | copy-start | bytes 786436
  71.2 10.0 %copy-start.4 = (bf16[8,64,256]{2,1,0:T(8,128)(2,1)}, bf16[8,64,256]{2,1,0:T(8,128)(2,1)S(1)}, u32[]{:S(2)}) copy-start(bf16[8,64,256]{2,1,0:T(8,128)(2,1)S(1)} %get-tuple-element.86) | copy-start | bytes 786436
  75.4 5.9 %copy-start.7 = (bf16[8,64,256]{2,1,0:T(8,128)(2,1)S(1)}, bf16[8,64,256]{2,1,0:T(8,128)(2,1)}, u32[]{:S(2)}) copy-start(bf16[8,64,256]{2,1,0:T(8,128)(2,1)} %copy-done.6) | copy-start | bytes 786436
  75.4 396.9 %all-to-all-start = ((f32[32,64,256]{2,1,0:T(8,128)}), f32[32,64,256]{2,1,0:T(8,128)S(1)}, u32[]{:S(2)}, u32[]{:S(2)}) async-start(f32[32,64,256]{2,1,0:T(8,128)} %broadcast_select_fusion), calls=%async_computation | async-start | bytes 4194304 | tf_op jit(solution)/shard_map/all_to_all | solution.py:268
  81.0 389.2 %all-reduce.22.cloned.1.call-start = ((), (), s32[]{:S(2)}) async-start(), calls=%async_computation.2 | async-start | bytes 1474560 | tf_op jit(solution)/shard_map/psum | solution.py:273
  105.7 4.7 copy-start.21
  111.8 4.8 copy-start.1
  111.8 4.8 copy-start.3
  111.8 4.7 copy-start.5
  111.8 4.7 copy-start.8
  112.7 102.8 %collective-permute-start.4 = (f32[64,1,130]{0,2,1:T(8,128)}, f32[64,1,130]{0,2,1:T(8,128)S(1)}, u32[]{:S(2)}, u32[]{:S(2)}) collective-permute-start(f32[64,1,130]{0,2,1:T(8,128)} %get-tuple-element.93), channel_id=1, source_target_pairs={{0,32},{32,64},{64,96},{96,128},{128,160},{160,192},{192,224},{224... | collective-permute-start | bytes 99848 | tf_op jit(solution)/shard_map/ppermute | solution.py:17
  112.7 102.8 %collective-permute-start.5 = (f32[64,1,130]{0,2,1:T(8,128)}, f32[64,1,130]{0,2,1:T(8,128)S(1)}, u32[]{:S(2)}, u32[]{:S(2)}) collective-permute-start(f32[64,1,130]{0,2,1:T(8,128)} %get-tuple-element.94), channel_id=1, source_target_pairs={{32,0},{64,32},{96,64},{128,96},{160,128},{192,160},{224,192},{0,2... | collective-permute-start | bytes 99848 | tf_op jit(solution)/shard_map/ppermute | solution.py:19
  215.6 171.3 %collective-permute-start.7 = (f32[64,20,1]{0,2,1:T(1,128)S(1)}, f32[64,20,1]{0,2,1:T(1,128)S(1)}, u32[]{:S(2)}, u32[]{:S(2)}) collective-permute-start(f32[64,20,1]{0,2,1:T(1,128)S(1)} %get-tuple-element.91), channel_id=1, source_target_pairs={{1,0},{2,1},{3,2},{4,3},{5,4},{6,5},{7,6},{8,7},{9,8},{10,9},{11,1... | collective-permute-start | bytes 15368 | tf_op jit(solution)/shard_map/ppermute | solution.py:19
  215.8 169.5 %collective-permute-start.6 = (f32[64,20,1]{0,2,1:T(1,128)S(1)}, f32[64,20,1]{0,2,1:T(1,128)S(1)}, u32[]{:S(2)}, u32[]{:S(2)}) collective-permute-start(f32[64,20,1]{0,2,1:T(1,128)S(1)} %get-tuple-element.92), channel_id=1, source_target_pairs={{0,1},{1,2},{2,3},{3,4},{4,5},{5,6},{6,7},{7,8},{8,9},{9,10},{10,1... | collective-permute-start | bytes 15368 | tf_op jit(solution)/shard_map/ppermute | solution.py:17
  (10 other events, 17.8 us)
Sparse Core Ops, SparseCore 0:
  73.2 311.9 all-reduce.19
  387.9 82.2 all-reduce.21
